TPU v7x, 128 devices: a whole 4x4x4 slice. The times are simulated.
128 devices in a mesh: wide: 16 (over y, x), narrow: 8 (over z, core).
Axes of the slice: x: 4, y: 4, z: 4, core: 2. Of those that a mesh axis runs over, the one named last changes fastest.
Arguments:
- diag_block: float32 [256, 256], P('narrow'), as said below
- panel_below: float32 [24576, 256], P(('wide', 'narrow')), may hold values from -0.216 to 0.216
- trailing_slab: float32 [12288, 24576], P('narrow', 'wide'), may hold values from -6 to 6
Outputs:
- updated: float32 [12288, 24576], P('narrow', 'wide')
Inputs may be any that keep to these rules, and one draw needn't show every extreme that they name: `diag_block`: symmetric positive definite; its smallest eigenvalue is 0.01 or more and its diagonal entries lie between 0.4 and 2.1.
All inputs are finite; a program needn't handle non-finite values.
Results may differ from a plain program's by a relative error of at most 0.00016.
Values sent between devices are 32-bit elements; how exact they have to be, the bound alone decides.
A program may use at most 64 MiB of HBM per device.

v0:
```python
import jax
import jax.numpy as jnp
from jax import lax
from jax.sharding import PartitionSpec as P

unit_gamma = 65538.0 * 2.0 ** (-24) / (1.0 - 65538.0 * 2.0 ** (-24))


def from_root(block, axis, source):
    block = jnp.where(lax.axis_index(axis) == source, block, jnp.zeros_like(block))
    return lax.psum(block, axis)


def factor_block(diag_full):
    trace_sum = jnp.sum(jnp.diagonal(diag_full))
    shift_value = unit_gamma * trace_sum / diag_full.shape[0]
    identity = jnp.eye(diag_full.shape[0], dtype=jnp.float32)
    return jnp.linalg.cholesky(diag_full - shift_value * identity)


def solve_rows(raw_panel, lower_factor):
    return jax.scipy.linalg.solve_triangular(lower_factor, raw_panel.T, lower=True).T


def on_device(diag_block, panel_below, trailing_slab):
    diag_full = lax.all_gather(diag_block, "narrow", axis=0, tiled=True)
    lower_factor = factor_block(diag_full)
    owner = lax.axis_index("narrow")
    solved_mine = solve_rows(panel_below, lower_factor)
    column_panel = lax.all_gather(solved_mine, "narrow", axis=0, tiled=True)
    row_panel = from_root(column_panel, "wide", owner)
    product = lax.dot_general(
        row_panel,
        column_panel,
        (((1,), (1,)), ((), ())),
        precision=lax.Precision.HIGHEST,
        preferred_element_type=jnp.float32,
    )
    return trailing_slab - product


def solution(mesh):
    placed = (P("narrow", None), P(("wide", "narrow"), None), P("narrow", "wide"))
    return jax.shard_map(
        on_device, mesh=mesh, in_specs=placed, out_specs=P("narrow", "wide"), check_vma=False
    )
```

profile of v0, /device:TPU:1, one launch (start us, length us, event | category | flops | bytes accessed | tf_op | source)
XLA Modules:
  0.0 223.1 jit_solution(3834586539519067064)
XLA Ops:
  6.5 0.0 all-gather.2.cloned.1.call-start
  6.6 15.6 %all_gather.6 = f32[256,256]{1,0:T(8,128)S(1)} all-gather(f32[32,256]{1,0:T(8,128)} %param.3), channel_id=1, replica_groups=mesh['wide'=16,'narrow'=8] {'narrow'}, dimensions={0}, use_global_device_ids=true | all-gather | bytes 294912 | tf_op jit(solution)/shard_map/all_gather | solution.py:26
  22.1 0.1 copy.23
  22.3 2.3 %gather_fusion = f32[256]{0:T(256)S(1)} fusion(f32[256,256]{1,0:T(8,128)S(1)} %all_gather.6, s32[256]{0:T(256)S(1)} %bitcast.35), kind=kCustom, calls=%fused_computation | custom fusion | bytes 4096 | tf_op jit(solution)/shard_map/jit(diagonal)/cond/branch_0_fun/gather | solution.py:15
  24.6 0.6 reduce_sum.9
  25.9 0.1 copy.24
  26.1 11.7 %cholesky.49 = f32[128,128]{1,0:T(8,128)S(1)} custom-call(f32[128,128]{1,0:T(8,128)S(1)} %cholesky.115), custom_call_target="Cholesky" | custom-call | tf_op jit(solution)/shard_map/jit(cholesky)/cholesky | solution.py:18
  37.8 0.1 copy.25
  38.0 9.8 %custom-call.15 = f32[1,128,128]{1,2,0:T(8,128)S(1)} custom-call(f32[1,128,128]{2,1,0:T(8,128)S(1)} %get-tuple-element.40), custom_call_target="InvertDiagBlocksLowerTriangular" | custom-call | tf_op jit(solution)/shard_map/jit(cholesky)/cholesky | solution.py:18
  47.8 0.2 fusion.5
  48.0 0.3 convolution_subtract_fusion.2
  48.3 0.1 copy.26
  48.4 11.7 %cholesky.103 = f32[128,128]{1,0:T(8,128)S(1)} custom-call(f32[128,128]{1,0:T(8,128)S(1)} %convolution_subtract_fusion.2), custom_call_target="Cholesky" | custom-call | tf_op jit(solution)/shard_map/jit(cholesky)/cholesky | solution.py:18
  60.1 0.1 copy.27
  60.2 0.0 copy-start.1
  60.3 0.7 compare_reduce_fusion
  62.3 0.1 triangular_solve.60
  62.4 4.3 %while.1 = (s32[]{:T(128)}, f32[256,256]{0,1:T(8,128)S(1)}, s32[2,2]{1,0:T(2,128)S(1)}, f32[2,128,128]{2,1,0:T(8,128)S(1)}, s32[]{:T(128)}) while((s32[]{:T(128)}, f32[256,256]{0,1:T(8,128)S(1)}, s32[2,2]{1,0:T(2,128)S(1)}, f32[2,128,128]{2,1,0:T(8,128)S(1)}, s32[]{:T(128)}) %tuple.25), condition=%wide.while_cond, body=%wide.while_body.sunk | while | flops 2 | bytes 393329 | solution.py:22
  62.4 0.7 fusion.16
  63.0 1.3 dynamic-slice.7
  64.4 0.1 copy.31
  64.5 0.7 fusion.16
  65.2 1.3 dynamic-slice.7
  66.5 0.1 copy.31
  66.7 19.9 %custom-call.16 = f32[2,128,128]{1,2,0:T(8,128)S(1)} custom-call(f32[2,128,128]{2,1,0:T(8,128)S(1)} %get-tuple-element.12), custom_call_target="InvertDiagBlocksLowerTriangular" | custom-call | tf_op jit(solution)/shard_map/jit(_solve_triangular)/triangular_solve | solution.py:22
  86.5 0.0 copy-done.1
  86.5 0.2 fusion.1
  86.8 0.2 convolution_subtract_fusion.1
  87.0 0.2 fusion.4
  87.3 0.7 maximum_bitcast_fusion
  88.0 0.0 all-gather.2.cloned.1.call-update
  88.0 0.0 all-reduce.3.cloned.1.call-start
  88.0 25.7 %all-gather.2.cloned.1.call-done = f32[1536,256]{1,0:T(8,128)} async-done(((f32[192,256]{1,0:T(8,128)}), f32[1536,256]{1,0:T(8,128)}) %all-gather.2.cloned.1.call-update) | async-done | bytes 1572880 | tf_op jit(solution)/shard_map/all_gather | solution.py:30
  113.8 1.2 broadcast_select_fusion
  115.0 0.0 copy-start
  115.0 0.0 all-reduce.3.cloned.1.call-update
  115.1 88.7 %all-reduce.3.cloned.1.call-done = f32[1536,256]{1,0:T(8,128)} async-done(((f32[1536,256]{1,0:T(8,128)}), f32[1536,256]{1,0:T(8,128)}) %all-reduce.3.cloned.1.call-update) | async-done | bytes 1572880 | tf_op jit(solution)/shard_map/psum | solution.py:11
  203.8 0.0 copy-done
  203.8 12.4 %convolution_subtract_fusion = f32[1536,1536]{1,0:T(8,128)} fusion(f32[1536,1536]{1,0:T(8,128)} %param.5, f32[1536,256]{1,0:T(8,128)} %all-reduce.3.cloned.1.call-done, f32[1536,256]{1,0:T(8,128)S(1)} %copy-done), kind=kOutput, calls=%fused_computation.3 | convolution fusion | flops 7250116608 | bytes 22020096 | tf_op jit(solution)/shard_map/dot_general | solution.py:32
  (16 shorter events, 0.3 us)
Async XLA Ops:
  6.5 107.3 %all-gather.2.cloned.1.call-start = ((), (), s32[]{:S(2)}) async-start(), calls=%async_computation | async-start | bytes 1769472 | tf_op jit(solution)/shard_map/all_gather | solution.py:30
  60.2 26.3 %copy-start.1 = (f32[192,256]{1,0:T(8,128)S(1)}, f32[192,256]{1,0:T(8,128)}, u32[]{:S(2)}) copy-start(f32[192,256]{1,0:T(8,128)} %param.4) | copy-start | bytes 589828
  88.0 115.8 %all-reduce.3.cloned.1.call-start = ((), (), s32[]{:S(2)}) async-start(), calls=%async_computation.1 | async-start | bytes 3145728 | tf_op jit(solution)/shard_map/psum | solution.py:11
  115.0 88.7 %copy-start = (f32[1536,256]{1,0:T(8,128)S(1)}, f32[1536,256]{1,0:T(8,128)}, u32[]{:S(2)}) copy-start(f32[1536,256]{1,0:T(8,128)} %all-gather.2.cloned.1.call-done) | copy-start | bytes 4718596
Sparse Core Ops, SparseCore 0:
  88.1 25.6 all-gather.1
  117.1 86.6 all-reduce.2
where the time goes:
time: 224 us; the launch traced here: 223 us
  waiting for transfers between devices  114 us (51%)
  other arithmetic  56.5 us (25%)
  blocking collectives  15.6 us (7%)
  between operations  15.5 us (7%)
  matrix products  13.6 us (6%)
  local copies, waits for them, and re-layouts  7.22 us (3%)
    psum x1, waiting for transfers between devices, from_root(): return lax.psum(block, axis)  88.7 us
    another operation x6, other arithmetic, factor_block(): return jnp.linalg.cholesky(diag_full - shift_value * identity)  34 us
    all_gather x1, waiting for transfers between devices, on_device(): column_panel = lax.all_gather(solved_mine, 'narrow', axis=0, tiled=True)  25.7 us
    another operation x3, other arithmetic, solve_rows(): jax.scipy.linalg.solve_triangular(lower_factor, raw_panel.T, lower=True)  19.9 us
    all_gather x1, blocking collectives, on_device(): diag_full = lax.all_gather(diag_block, 'narrow', axis=0, tiled=True)  15.6 us
    dot_general x1, matrix products, on_device(): lax.dot_general(row_panel, column_panel, (((1,), (1,)), ((), ())), precis...  12.4 us
  transfers between devices with their start and end apart: 2, of which 2 were waited for; matrix products, arithmetic and copies ran while one was open for 0% of the time, Pallas kernels for 0%

commit v1 on v0

v1 whole, which is shorter than its diff:
```python
import functools

import jax
import jax.numpy as jnp
from jax import lax
from jax.experimental import pallas as pl
from jax.experimental.pallas import tpu as pltpu
from jax.sharding import PartitionSpec as P

unit_gamma = 65538.0 * 2.0 ** (-24) / (1.0 - 65538.0 * 2.0 ** (-24))
MESH = pl.DeviceIdType.MESH
LAST = (((1,), (1,)), ((), ()))
PLAIN = (((1,), (0,)), ((), ()))


def full_dot(a, b, dims):
    return lax.dot_general(
        a, b, dims, precision=lax.Precision.HIGHEST, preferred_element_type=jnp.float32
    )


def half_dot(a, b, dims):
    return lax.dot_general(a, b, dims, preferred_element_type=jnp.float32)


def halves(x):
    high = x.astype(jnp.bfloat16)
    low = (x - high.astype(jnp.float32)).astype(jnp.bfloat16)
    return high, low


def eliminate(m_ref, out_ref):
    count = 16
    lane = lax.broadcasted_iota(jnp.int32, (8, 128), 1)
    sub = lax.broadcasted_iota(jnp.int32, (8, 128), 0)
    blocks = [m_ref[8 * i : 8 * i + 8, :] for i in range(count)]
    for j in range(count):
        first = 8 * j
        block = blocks[j]
        inside = (lane >= first) & (lane < first + 8)
        a, e = {}, {}
        for q in range(8):
            column = jnp.broadcast_to(block[:, first + q : first + q + 1], (8, 128))
            for p in range(q, 8):
                a[p, q] = jnp.broadcast_to(column[p : p + 1, :], (8, 128))
        eye = (lane - first == sub).astype(jnp.float32)
        placed = jnp.where(inside, eye, block)
        lead = [jnp.broadcast_to(placed[m : m + 1, :], (8, 128)) for m in range(8)]
        inverse = [None] * 8
        for k in range(8):
            inverse[k] = 1.0 / a[k, k]
            for i in range(k + 1, 8):
                factor = a[i, k] * inverse[k]
                for q in range(k + 1, i + 1):
                    a[i, q] = a[i, q] - factor * a[q, k]
                lead[i] = lead[i] - factor * lead[k]
                for q in range(k):
                    e[i, q] = e[i, q] - factor * e[k, q]
                e[i, k] = -factor
        scaled = [inverse[m] * lead[m] for m in range(8)]
        solved = list(scaled)
        for m in range(8):
            for n in range(m + 1, 8):
                solved[m] = solved[m] + e[n, m] * scaled[n]
        rows = lead[0] * lax.rsqrt(a[0, 0])
        for m in range(1, 8):
            rows = jnp.where(sub == m, lead[m] * lax.rsqrt(a[m, m]), rows)
        out_ref[first : first + 8, :] = jnp.where(lane <= sub + first, rows, 0.0)
        for i in range(j + 1, count):
            below = blocks[i]
            total = jnp.where(inside, 0.0, below)
            for m in range(8):
                weight = jnp.broadcast_to(below[:, first + m : first + m + 1], (8, 128))
                total = total - weight * solved[m]
            blocks[i] = total


def gather_kernel(
    diag_ref, panel_ref, row_ref, col_ref,
    diag_all, col_all, row_all, work, inv,
    diag_send, diag_recv, col_send, col_recv, part_send, part_recv, row_send, row_recv,
):
    w, n = lax.axis_index("wide"), lax.axis_index("narrow")
    wides, narrows = 16, 8
    part = panel_ref.shape[0] // 2
    piece = lax.rem(w + 12, wides)
    source = (n, lax.div(piece, 2))
    barrier = pltpu.get_barrier_semaphore()

    def target(half):
        return (lax.rem(2 * n + half + 4, wides), w)

    def signal(device):
        pl.semaphore_signal(barrier, inc=1, device_id=device, device_id_type=MESH)

    for step in range(1, narrows):
        signal((w, lax.rem(n + step, narrows)))
    for step in range(1, wides):
        signal((lax.rem(w + step, wides), n))
    signal(source)

    @pl.when(w < narrows)
    def _():
        signal(target(0))
        signal(target(1))

    diag_all[n] = diag_ref[...]
    col_all[n] = panel_ref[...]
    peers = narrows + wides - 1

    @pl.when(w < narrows)
    def _():
        pl.semaphore_wait(barrier, peers + 2)

    @pl.when(w >= narrows)
    def _():
        pl.semaphore_wait(barrier, peers)

    def diag_copy(step):
        return pltpu.make_async_remote_copy(
            diag_ref, diag_all.at[n], diag_send.at[step], diag_recv.at[step],
            device_id=(w, lax.rem(n + step, narrows)), device_id_type=MESH)

    def col_copy(step):
        return pltpu.make_async_remote_copy(
            panel_ref, col_all.at[n], col_send.at[step], col_recv.at[step],
            device_id=(w, lax.rem(n + step, narrows)), device_id_type=MESH)

    def part_copy(half):
        return pltpu.make_async_remote_copy(
            panel_ref.at[pl.ds(part * half, part)], row_all.at[2 * n + half],
            part_send.at[half], part_recv.at[0],
            device_id=target(half), device_id_type=MESH)

    def row_copy(step):
        return pltpu.make_async_remote_copy(
            row_all.at[piece], row_all.at[piece], row_send.at[step], row_recv.at[step],
            device_id=(lax.rem(w + step, wides), n), device_id_type=MESH)

    for step in range(1, narrows):
        diag_copy(step).start()

    @pl.when(w < narrows)
    def _():
        part_copy(0).start()
        part_copy(1).start()

    for step in range(1, narrows):
        col_copy(step).start()
    part_copy(0).wait_recv()
    for step in range(1, wides):
        row_copy(step).start()
    for step in range(1, narrows):
        diag_copy(step).wait_recv()

    row_id = lax.broadcasted_iota(jnp.int32, (32, 256), 0)
    col_id = lax.broadcasted_iota(jnp.int32, (32, 256), 1)
    trace = jnp.zeros((32, 256), jnp.float32)
    for i in range(narrows):
        trace = trace + jnp.where(col_id == row_id + 32 * i, diag_all[i], 0.0)
    shift = unit_gamma * jnp.sum(trace, keepdims=True) / 256.0
    for i in range(narrows):
        work[32 * i : 32 * i + 32, :] = jnp.where(
            col_id == row_id + 32 * i, diag_all[i] - shift, diag_all[i])
    eliminate(work.at[0:128, 0:128], inv.at[0:128, 0:128])
    inv[0:128, 128:256] = jnp.zeros((128, 128), jnp.float32)
    first = inv[0:128, 0:128]
    below = full_dot(work[128:256, 0:128], first, LAST)
    beside = full_dot(first, work[0:128, 128:256], PLAIN)
    work[128:256, 128:256] = work[128:256, 128:256] - full_dot(below, beside, PLAIN)
    eliminate(work.at[128:256, 128:256], inv.at[128:256, 128:256])
    inv[128:256, 0:128] = -full_dot(
        inv[128:256, 128:256], full_dot(below, first, PLAIN), PLAIN)

    inv_high, inv_low = halves(inv[...])

    def solve(raw, out_ref, start):
        high, low = halves(raw)
        done = (half_dot(high, inv_high, LAST) + half_dot(high, inv_low, LAST)
                + half_dot(low, inv_high, LAST))
        high, low = halves(done)
        out_ref[pl.ds(start, raw.shape[0]), 0:256] = high
        out_ref[pl.ds(start, raw.shape[0]), 256:512] = low

    for step in range(1, narrows):
        col_copy(step).wait_recv()

    @pl.loop(0, narrows)
    def _(i):
        solve(col_all[i], col_ref, pl.multiple_of(i * 192, 192))

    for step in range(1, wides):
        row_copy(step).wait_recv()

    @pl.loop(0, wides)
    def _(i):
        solve(row_all[i], row_ref, pl.multiple_of(i * 96, 96))

    for step in range(1, narrows):
        diag_copy(step).wait_send()
        col_copy(step).wait_send()
    for step in range(1, wides):
        row_copy(step).wait_send()

    @pl.when(w < narrows)
    def _():
        part_copy(0).wait_send()
        part_copy(1).wait_send()


def gather_and_solve(diag_block, panel_below):
    rows = panel_below.shape[0]
    vmem = pl.BlockSpec(memory_space=pltpu.VMEM)
    out = jax.ShapeDtypeStruct((8 * rows, 512), jnp.bfloat16)
    sems = pltpu.SemaphoreType.DMA
    return pl.pallas_call(
        gather_kernel,
        out_shape=(out, out),
        in_specs=[vmem, vmem],
        out_specs=(vmem, vmem),
        scratch_shapes=[
            pltpu.VMEM((8, 32, 256), jnp.float32),
            pltpu.VMEM((8, rows, 256), jnp.float32),
            pltpu.VMEM((16, rows // 2, 256), jnp.float32),
            pltpu.VMEM((256, 256), jnp.float32),
            pltpu.VMEM((256, 256), jnp.float32),
            sems((8,)), sems((8,)), sems((8,)), sems((8,)),
            sems((2,)), sems((1,)), sems((16,)), sems((16,)),
        ],
        compiler_params=pltpu.CompilerParams(
            collective_id=0, has_side_effects=True, vmem_limit_bytes=24 << 20),
        name="gather_and_solve",
    )(diag_block, panel_below)


def update_kernel(row_ref, col_ref, slab_ref, out_ref):
    high, low = row_ref[:, 0:256], row_ref[:, 256:512]
    col_high, col_low = col_ref[:, 0:256], col_ref[:, 256:512]
    product = (half_dot(high, col_high, LAST) + half_dot(high, col_low, LAST)
               + half_dot(low, col_high, LAST))
    out_ref[...] = slab_ref[...] - product


def update(row_panel, col_panel, slab):
    rows, cols = slab.shape
    tile = 256
    return pl.pallas_call(
        update_kernel,
        out_shape=jax.ShapeDtypeStruct(slab.shape, jnp.float32),
        grid=(rows // tile,),
        in_specs=[
            pl.BlockSpec((tile, 512), lambda i: (i, 0)),
            pl.BlockSpec((cols, 512), lambda i: (0, 0)),
            pl.BlockSpec((tile, cols), lambda i: (i, 0)),
        ],
        out_specs=pl.BlockSpec((tile, cols), lambda i: (i, 0)),
        compiler_params=pltpu.CompilerParams(vmem_limit_bytes=32 << 20),
        name="update",
    )(row_panel, col_panel, slab)


def on_device(diag_block, panel_below, trailing_slab):
    row_panel, col_panel = gather_and_solve(diag_block, panel_below)
    return update(row_panel, col_panel, trailing_slab)


def solution(mesh):
    placed = (P("narrow", None), P(("wide", "narrow"), None), P("narrow", "wide"))
    return jax.shard_map(
        on_device, mesh=mesh, in_specs=placed, out_specs=P("narrow", "wide"), check_vma=False
    )
```

time: 224 us -> 60.5 us (0.27)
  the two profiles are of different devices: /device:TPU:1 before, /device:TPU:19 now
where the time goes in v1:
time: 60.5 us; the launch traced here: 60.3 us
  Pallas kernels  54.9 us (91%)
  local copies, waits for them, and re-layouts  5.36 us (9%)
    pallas_call x1, Pallas kernels, gather_and_solve(): pl.pallas_call(gather_kernel, out_shape=(out, out), in_specs=[vmem, vmem]...  48.3 us
    pallas_call x1, Pallas kernels, update(): pl.pallas_call(update_kernel, out_shape=jax.ShapeDtypeStruct(slab.shape,...  6.66 us
    unnamed x6, local copies, waits for them, and re-layouts  5.36 us

profile of v1, /device:TPU:19, one launch (start us, length us, event | category | flops | bytes accessed | tf_op | source)
XLA Modules:
  0.0 60.3 jit_solution(7356989844050935042)
XLA Ops:
  0.0 0.0 copy-start.1
  0.0 0.9 %copy-done.1 = f32[192,256]{1,0:T(8,128)S(1)} copy-done((f32[192,256]{1,0:T(8,128)S(1)}, f32[192,256]{1,0:T(8,128)}, u32[]{:S(2)}) %copy-start.1) | copy-done | bytes 196632
  0.9 0.0 copy-start.2
  0.9 0.8 %copy-done.2 = f32[32,256]{1,0:T(8,128)S(1)} copy-done((f32[32,256]{1,0:T(8,128)S(1)}, f32[32,256]{1,0:T(8,128)}, u32[]{:S(2)}) %copy-start.2) | copy-done | bytes 32792
  1.7 48.3 %gather_and_solve.1 = (bf16[1536,512]{1,0:T(8,128)(2,1)S(1)}, bf16[1536,512]{1,0:T(8,128)(2,1)S(1)}) custom-call(f32[32,256]{1,0:T(8,128)S(1)} %copy-done.2, f32[192,256]{1,0:T(8,128)S(1)} %copy-done.1), custom_call_target="tpu_custom_call" | custom-call | tf_op jit(solution)/shard_map/gather_and_solve/pallas_call | solution.py:216
  50.0 0.0 copy-start
  50.0 3.7 %copy-done = f32[1536,1536]{1,0:T(8,128)S(1)} copy-done((f32[1536,1536]{1,0:T(8,128)S(1)}, f32[1536,1536]{1,0:T(8,128)}, u32[]{:S(2)}) %copy-start) | copy-done | bytes 9437208
  53.6 6.7 %update.1 = f32[1536,1536]{1,0:T(8,128)} custom-call(bf16[1536,512]{1,0:T(8,128)(2,1)S(1)} %get-tuple-element.7.row_ref, bf16[1536,512]{1,0:T(8,128)(2,1)S(1)} %get-tuple-element.8.col_ref, f32[1536,1536]{1,0:T(8,128)S(1)} %copy-done), custom_call_target="tpu_custom_call" | custom-call | tf_op jit(solution)/shard_map/update/pallas_call | solution.py:247
Async XLA Ops:
  0.0 0.9 %copy-start.1 = (f32[192,256]{1,0:T(8,128)S(1)}, f32[192,256]{1,0:T(8,128)}, u32[]{:S(2)}) copy-start(f32[192,256]{1,0:T(8,128)} %panel_ref.1) | copy-start | bytes 589828
  0.9 0.8 %copy-start.2 = (f32[32,256]{1,0:T(8,128)S(1)}, f32[32,256]{1,0:T(8,128)}, u32[]{:S(2)}) copy-start(f32[32,256]{1,0:T(8,128)} %diag_ref.1) | copy-start | bytes 98308
  50.0 3.7 %copy-start = (f32[1536,1536]{1,0:T(8,128)S(1)}, f32[1536,1536]{1,0:T(8,128)}, u32[]{:S(2)}) copy-start(f32[1536,1536]{1,0:T(8,128)} %slab_ref.1) | copy-start | bytes 28311556

commit v2 on v1

v2 whole, which is shorter than its diff:
```python
import functools

import jax
import jax.numpy as jnp
from jax import lax
from jax.experimental import pallas as pl
from jax.experimental.pallas import tpu as pltpu
from jax.sharding import PartitionSpec as P

unit_gamma = 65538.0 * 2.0 ** (-24) / (1.0 - 65538.0 * 2.0 ** (-24))
MESH = pl.DeviceIdType.MESH
PHASE_TWO, TWIN = 6, 4
LAST = (((1,), (1,)), ((), ()))
PLAIN = (((1,), (0,)), ((), ()))


def full_dot(a, b, dims):
    return lax.dot_general(
        a, b, dims, precision=lax.Precision.HIGHEST, preferred_element_type=jnp.float32
    )


def half_dot(a, b, dims):
    return lax.dot_general(a, b, dims, preferred_element_type=jnp.float32)


def halves(x):
    high = x.astype(jnp.bfloat16)
    low = (x - high.astype(jnp.float32)).astype(jnp.bfloat16)
    return high, low


def eliminate(m_ref, out_ref, errands=None):
    count = 16
    lane = lax.broadcasted_iota(jnp.int32, (8, 128), 1)
    sub = lax.broadcasted_iota(jnp.int32, (8, 128), 0)
    blocks = [m_ref[8 * i : 8 * i + 8, :] for i in range(count)]
    for j in range(count):
        if errands and j in errands:
            errands[j]()
        first = 8 * j
        block = blocks[j]
        inside = (lane >= first) & (lane < first + 8)
        a, e = {}, {}
        for q in range(8):
            column = jnp.broadcast_to(block[:, first + q : first + q + 1], (8, 128))
            for p in range(q, 8):
                a[p, q] = jnp.broadcast_to(column[p : p + 1, :], (8, 128))
        eye = (lane - first == sub).astype(jnp.float32)
        placed = jnp.where(inside, eye, block)
        lead = [jnp.broadcast_to(placed[m : m + 1, :], (8, 128)) for m in range(8)]
        inverse = [None] * 8
        for k in range(8):
            inverse[k] = 1.0 / a[k, k]
            for i in range(k + 1, 8):
                factor = a[i, k] * inverse[k]
                for q in range(k + 1, i + 1):
                    a[i, q] = a[i, q] - factor * a[q, k]
                lead[i] = lead[i] - factor * lead[k]
                for q in range(k):
                    e[i, q] = e[i, q] - factor * e[k, q]
                e[i, k] = -factor
        scaled = [inverse[m] * lead[m] for m in range(8)]
        solved = list(scaled)
        for m in range(8):
            for n in range(m + 1, 8):
                solved[m] = solved[m] + e[n, m] * scaled[n]
        rows = lead[0] * lax.rsqrt(a[0, 0])
        for m in range(1, 8):
            rows = jnp.where(sub == m, lead[m] * lax.rsqrt(a[m, m]), rows)
        out_ref[first : first + 8, :] = jnp.where(lane <= sub + first, rows, 0.0)
        for i in range(j + 1, count):
            below = blocks[i]
            total = jnp.where(inside, 0.0, below)
            for m in range(8):
                weight = jnp.broadcast_to(below[:, first + m : first + m + 1], (8, 128))
                total = total - weight * solved[m]
            blocks[i] = total


def gather_kernel(
    diag_hbm, panel_hbm, slab_hbm, row_ref, col_ref, slab_ref,
    diag_all, traces, col_all, row_a, row_b, work, inv,
    local_sem, diag_send, diag_recv, rest_send, rest_recv, col_send, col_recv,
    twin_send, twin_recv, part_send, part_recv, one_send, one_recv, two_send, two_recv,
):
    w, n = lax.axis_index("wide"), lax.axis_index("narrow")
    y, x = lax.div(w, 4), lax.rem(w, 4)
    z, core = lax.div(n, 2), lax.rem(n, 2)
    piece = lax.rem(w + 12, 16)
    piece_y, piece_x = lax.div(piece, 4), lax.rem(piece, 4)
    slot_a, slot_b = 4 * piece_y + piece_x, 4 * piece_x + piece_y
    twin = (w, 2 * z + 1 - core)

    def along_x(step):
        return (4 * y + lax.rem(x + step, 4), n)

    def along_y(step):
        return (4 * lax.rem(y + step, 4) + x, n)

    def along_z(step):
        return (w, 2 * lax.rem(z + step, 4) + core)

    def target(half):
        return (lax.rem(2 * n + half + 4, 16), w)

    source = (n, lax.div(piece, 2))

    slab_copy = pltpu.make_async_copy(slab_hbm, slab_ref, local_sem.at[0])
    diag_own = pltpu.make_async_copy(
        diag_hbm, diag_all.at[pl.ds(pl.multiple_of(32 * n, 32), 32)], local_sem.at[1])
    panel_own = pltpu.make_async_copy(
        panel_hbm, col_all.at[pl.ds(pl.multiple_of(192 * n, 64), 192)], local_sem.at[2])
    diag_own.start()
    panel_own.start()

    barrier = pltpu.get_barrier_semaphore()

    def signal(device):
        pl.semaphore_signal(barrier, inc=1, device_id=device, device_id_type=MESH)

    for step in range(1, 8):
        signal((w, lax.rem(n + step, 8)))
    for step in range(1, 4):
        signal(along_x(step))
        signal(along_y(step))
    signal(source)

    @pl.when(w < 8)
    def _():
        signal(target(0))
        signal(target(1))

    slab_copy.start()
    diag_own.wait()
    row_id = lax.broadcasted_iota(jnp.int32, (32, 256), 0)
    col_id = lax.broadcasted_iota(jnp.int32, (32, 256), 1)
    own = diag_all[pl.ds(pl.multiple_of(32 * n, 32), 32), :]
    own = jnp.where(col_id == row_id + 32 * n, own, 0.0)
    own = own[:, 0:128] + own[:, 128:256]
    traces[n] = jnp.sum(own, axis=0, keepdims=True)

    @pl.when(w < 8)
    def _():
        pl.semaphore_wait(barrier, 16)

    @pl.when(w >= 8)
    def _():
        pl.semaphore_wait(barrier, 14)

    def remote(src, dst, send, recv, device):
        return pltpu.make_async_remote_copy(
            src, dst, send, recv, device_id=device, device_id_type=MESH)

    def corner_copy(step, origin):
        block = diag_all.at[pl.ds(pl.multiple_of(32 * origin, 32), 32), 0:128]
        return remote(block, block, diag_send.at[step], diag_recv.at[origin],
                      (w, lax.rem(n + step, 8)))

    def trace_copy(step, origin):
        return remote(traces.at[origin], traces.at[origin], diag_send.at[step],
                      diag_recv.at[origin], (w, lax.rem(n + step, 8)))

    def rest_copy(step, origin):
        block = diag_all.at[pl.ds(pl.multiple_of(32 * origin, 32), 32)]
        return remote(block, block, rest_send.at[step], rest_recv.at[origin],
                      (w, lax.rem(n + step, 8)))

    def part_copy(half, side):
        p = 2 * n + half
        p_y, p_x = lax.div(p, 4), lax.rem(p, 4)
        place = 48 * (4 * p_x + p_y if side else 4 * p_y + p_x)
        return remote(
            col_all.at[pl.ds(pl.multiple_of(192 * n + 96 * half + 48 * side, 48), 48)],
            (row_b if side else row_a).at[pl.ds(pl.multiple_of(place, 48), 48)],
            part_send.at[2 * half + side], part_recv.at[side], target(half))

    def one_copy(step, side):
        buffer, slot = (row_b, slot_b) if side else (row_a, slot_a)
        block = buffer.at[pl.ds(pl.multiple_of(48 * slot, 48), 48)]
        return remote(block, block, one_send.at[side, step], one_recv.at[side, step],
                      along_y(step) if side else along_x(step))

    def two_copy(step, side):
        buffer, slot = (row_b, piece_x) if side else (row_a, piece_y)
        block = buffer.at[pl.ds(pl.multiple_of(192 * slot, 192), 192)]
        return remote(block, block, two_send.at[side, step], two_recv.at[side, step],
                      along_x(step) if side else along_y(step))

    def col_copy(step):
        block = col_all.at[pl.ds(pl.multiple_of(192 * n, 64), 192)]
        return remote(block, block, col_send.at[step], col_recv.at[step], along_z(step))

    def twin_copy(step):
        origin = 2 * lax.rem(z + 4 - step, 4) + core
        block = col_all.at[pl.ds(pl.multiple_of(192 * origin, 64), 192)]
        return remote(block, block, twin_send.at[step], twin_recv.at[step], twin)

    @pl.when(n < 4)
    def _():
        for step in range(1, 8):
            corner_copy(step, n).start()

    @pl.when(n >= 4)
    def _():
        for step in range(1, 8):
            trace_copy(step, n).start()

    panel_own.wait()

    @pl.when(w < 8)
    def _():
        for half in range(2):
            for side in range(2):
                part_copy(half, side).start()

    @pl.when(n >= 4)
    def _():
        for step in range(1, 8):
            rest_copy(step, n).start()

    for side in range(2):
        part_copy(0, side).wait_recv()
    for step in range(1, 4):
        one_copy(step, 0).start()
        one_copy(step, 1).start()
    for step in range(1, 4):
        col_copy(step).start()
    twin_copy(0).start()

    for origin in range(4):
        @pl.when(n != origin)
        def _():
            corner_copy(1, origin).wait_recv()
    for origin in range(4, 8):
        @pl.when(n != origin)
        def _():
            trace_copy(1, origin).wait_recv()

    total = jnp.zeros((8, 128), jnp.float32)
    sub = lax.broadcasted_iota(jnp.int32, (8, 128), 0)
    lane = lax.broadcasted_iota(jnp.int32, (8, 128), 1)
    for i in range(16):
        total = total + jnp.where(lane == sub + 8 * i, diag_all[8 * i : 8 * i + 8, 0:128], 0.0)
    total = jnp.sum(total, axis=0, keepdims=True)
    for i in range(4, 8):
        total = total + traces[i]
    shift = unit_gamma * jnp.sum(total, axis=1, keepdims=True) / 256.0

    def shifted(start):
        for i in range(16):
            block = diag_all[start + 8 * i : start + 8 * i + 8, start : start + 128]
            work[start + 8 * i : start + 8 * i + 8, :] = jnp.where(
                lane == sub + 8 * i, block - shift, block)

    def second_phase():
        for side in range(2):
            for step in range(1, 4):
                one_copy(step, side).wait_recv()
        for step in range(1, 4):
            two_copy(step, 0).start()
            two_copy(step, 1).start()

    def to_twin():
        for step in range(1, 4):
            col_copy(step).wait_recv()
            twin_copy(step).start()

    shifted(0)
    eliminate(work.at[0:128], inv.at[0:128, 0:128], {PHASE_TWO: second_phase})
    inv[0:128, 128:256] = jnp.zeros((128, 128), jnp.float32)
    for origin in range(4, 8):
        @pl.when(n != origin)
        def _():
            rest_copy(1, origin).wait_recv()
    shifted(128)
    first = inv[0:128, 0:128]
    corner = diag_all[128:256, 0:128]
    below = full_dot(corner, first, LAST)
    beside = full_dot(first, corner, LAST)
    work[128:256, :] = work[128:256, :] - full_dot(below, beside, PLAIN)
    eliminate(work.at[128:256], inv.at[128:256, 128:256], {TWIN: to_twin})
    inv[128:256, 0:128] = -full_dot(
        inv[128:256, 128:256], full_dot(below, first, PLAIN), PLAIN)

    inv_high, inv_low = halves(inv[...])

    def solve(raw):
        high, low = halves(raw)
        return halves(half_dot(high, inv_high, LAST) + half_dot(high, inv_low, LAST)
                      + half_dot(low, inv_high, LAST))

    for step in range(4):
        twin_copy(step).wait_recv()
    for start in (0, 768):
        high, low = solve(col_all[start : start + 768, :])
        col_ref[start : start + 768, 0:256] = high
        col_ref[start : start + 768, 256:512] = low
    for side in range(2):
        for step in range(1, 4):
            two_copy(step, side).wait_recv()
        high, low = solve((row_b if side else row_a)[...])
        for slot in range(16):
            place = 96 * (4 * (slot % 4) + slot // 4) + 48 if side else 96 * slot
            row_ref[place : place + 48, 0:256] = high[48 * slot : 48 * slot + 48]
            row_ref[place : place + 48, 256:512] = low[48 * slot : 48 * slot + 48]

    @pl.when(n < 4)
    def _():
        for step in range(1, 8):
            corner_copy(step, n).wait_send()

    @pl.when(n >= 4)
    def _():
        for step in range(1, 8):
            trace_copy(step, n).wait_send()
            rest_copy(step, n).wait_send()

    @pl.when(w < 8)
    def _():
        for half in range(2):
            for side in range(2):
                part_copy(half, side).wait_send()

    for step in range(1, 4):
        for side in range(2):
            one_copy(step, side).wait_send()
            two_copy(step, side).wait_send()
        col_copy(step).wait_send()
    for step in range(4):
        twin_copy(step).wait_send()
    slab_copy.wait()


def gather_and_solve(diag_block, panel_below, slab):
    rows = panel_below.shape[0]
    vmem = pl.BlockSpec(memory_space=pltpu.VMEM)
    hbm = pl.BlockSpec(memory_space=pltpu.HBM)
    out = jax.ShapeDtypeStruct((8 * rows, 512), jnp.bfloat16)
    sems = pltpu.SemaphoreType.DMA
    return pl.pallas_call(
        gather_kernel,
        out_shape=(out, out, jax.ShapeDtypeStruct(slab.shape, slab.dtype)),
        in_specs=[hbm, hbm, hbm],
        out_specs=(vmem, vmem, vmem),
        scratch_shapes=[
            pltpu.VMEM((256, 256), jnp.float32),
            pltpu.VMEM((8, 1, 128), jnp.float32),
            pltpu.VMEM((8 * rows, 256), jnp.float32),
            pltpu.VMEM((4 * rows, 256), jnp.float32),
            pltpu.VMEM((4 * rows, 256), jnp.float32),
            pltpu.VMEM((256, 128), jnp.float32),
            pltpu.VMEM((256, 256), jnp.float32),
            sems((3,)), sems((8,)), sems((8,)), sems((8,)), sems((8,)), sems((4,)), sems((4,)),
            sems((4,)), sems((4,)), sems((4,)), sems((2,)), sems((2, 4)), sems((2, 4)),
            sems((2, 4)), sems((2, 4)),
        ],
        compiler_params=pltpu.CompilerParams(
            collective_id=0, has_side_effects=True, vmem_limit_bytes=28 << 20),
        name="gather_and_solve",
    )(*(pltpu.with_memory_space_constraint(a, pltpu.HBM) for a in (diag_block, panel_below, slab)))


def update_kernel(row_ref, col_ref, slab_ref, out_hbm, buffer, sem):
    rows, cols = slab_ref.shape
    tall, broad, depth = 768, 512, 3
    tiles = [(i, j) for i in range(0, rows, tall) for j in range(0, cols, broad)]

    def out_copy(t):
        i, j = tiles[t]
        return pltpu.make_async_copy(
            buffer.at[t % depth], out_hbm.at[pl.ds(i, tall), pl.ds(j, broad)], sem.at[t % depth])

    for t, (i, j) in enumerate(tiles):
        if t >= depth:
            out_copy(t - depth).wait()
        high, low = row_ref[i : i + tall, 0:256], row_ref[i : i + tall, 256:512]
        col_high, col_low = col_ref[j : j + broad, 0:256], col_ref[j : j + broad, 256:512]
        product = (half_dot(high, col_high, LAST) + half_dot(high, col_low, LAST)
                   + half_dot(low, col_high, LAST))
        buffer[t % depth] = slab_ref[i : i + tall, j : j + broad] - product
        out_copy(t).start()
    for t in range(len(tiles) - depth, len(tiles)):
        out_copy(t).wait()


def update(row_panel, col_panel, slab):
    vmem = pl.BlockSpec(memory_space=pltpu.VMEM)
    return pl.pallas_call(
        update_kernel,
        out_shape=jax.ShapeDtypeStruct(slab.shape, jnp.float32),
        in_specs=[vmem, vmem, vmem],
        out_specs=pl.BlockSpec(memory_space=pltpu.HBM),
        scratch_shapes=[pltpu.VMEM((3, 768, 512), jnp.float32), pltpu.SemaphoreType.DMA((3,))],
        compiler_params=pltpu.CompilerParams(vmem_limit_bytes=24 << 20),
        name="update",
    )(row_panel, col_panel, slab)


def on_device(diag_block, panel_below, trailing_slab):
    row_panel, col_panel, slab = gather_and_solve(diag_block, panel_below, trailing_slab)
    return update(row_panel, col_panel, slab)


def solution(mesh):
    placed = (P("narrow", None), P(("wide", "narrow"), None), P("narrow", "wide"))
    return jax.shard_map(
        on_device, mesh=mesh, in_specs=placed, out_specs=P("narrow", "wide"), check_vma=False
    )
```

time: 60.5 us -> 41 us (0.68)
  the two profiles are of different devices: /device:TPU:19 before, /device:TPU:1 now
where the time goes in v2:
time: 41 us; the launch traced here: 40.9 us
  Pallas kernels  40.9 us (100%)
    pallas_call x1, Pallas kernels, gather_and_solve(): pl.pallas_call(gather_kernel, out_shape=(out, out, jax.ShapeDtypeStruct(s...  35.2 us
    pallas_call x1, Pallas kernels, update(): pl.pallas_call(update_kernel, out_shape=jax.ShapeDtypeStruct(slab.shape,...  5.62 us

profile of v2, /device:TPU:1, one launch (start us, length us, event | category | flops | bytes accessed | tf_op | source)
XLA Modules:
  0.0 40.9 jit_solution(10003540404969543123)
XLA Ops:
  0.0 35.2 %gather_and_solve.1 = (bf16[1536,512]{1,0:T(8,128)(2,1)S(1)}, bf16[1536,512]{1,0:T(8,128)(2,1)S(1)}, f32[1536,1536]{1,0:T(8,128)S(1)}) custom-call(f32[32,256]{1,0:T(8,128)} %diag_hbm.1, f32[192,256]{1,0:T(8,128)} %panel_hbm.1, f32[1536,1536]{1,0:T(8,128)} %slab_hbm.1), custom_call_target="tpu_custom_call" | custom-call | tf_op jit(solution)/shard_map/gather_and_solve/pallas_call | solution.py:341
  35.2 5.6 %update.1 = f32[1536,1536]{1,0:T(8,128)} custom-call(bf16[1536,512]{1,0:T(8,128)(2,1)S(1)} %get-tuple-element.8.row_ref, bf16[1536,512]{1,0:T(8,128)(2,1)S(1)} %get-tuple-element.9.col_ref, f32[1536,1536]{1,0:T(8,128)S(1)} %get-tuple-element.10.slab_ref), custom_call_target="tpu_custom_call" | custom-call | tf_op jit(solution)/shard_map/update/pallas_call | solution.py:389

commit v3 on v2

--- a/solution.py
+++ b/solution.py
@@ -9,7 +9,7 @@
 
 unit_gamma = 65538.0 * 2.0 ** (-24) / (1.0 - 65538.0 * 2.0 ** (-24))
 MESH = pl.DeviceIdType.MESH
-PHASE_TWO, TWIN = 6, 4
+PHASE_TWO, PHASE_THREE, TWIN, COLS_FIRST = 6, 4, 8, False
 LAST = (((1,), (1,)), ((), ()))
 PLAIN = (((1,), (0,)), ((), ()))
 
@@ -83,13 +83,17 @@
     diag_all, traces, col_all, row_a, row_b, work, inv,
     local_sem, diag_send, diag_recv, rest_send, rest_recv, col_send, col_recv,
     twin_send, twin_recv, part_send, part_recv, one_send, one_recv, two_send, two_recv,
+    relay_send, relay_recv,
 ):
     w, n = lax.axis_index("wide"), lax.axis_index("narrow")
     y, x = lax.div(w, 4), lax.rem(w, 4)
     z, core = lax.div(n, 2), lax.rem(n, 2)
-    piece = lax.rem(w + 12, 16)
-    piece_y, piece_x = lax.div(piece, 4), lax.rem(piece, 4)
-    slot_a, slot_b = 4 * piece_y + piece_x, 4 * piece_x + piece_y
+
+    def piece_at(col, row):
+        dx, dy = lax.rem(col + 4 - lax.rem(n, 4), 4), lax.rem(row + 4 - lax.div(n, 4), 4)
+        return 4 * lax.rem(dx + dy + z + 2, 4) + dy
+
+    ahead = 1 + 2 * core
     twin = (w, 2 * z + 1 - core)
 
     def along_x(step):
@@ -102,9 +106,11 @@
         return (w, 2 * lax.rem(z + step, 4) + core)
 
     def target(half):
-        return (lax.rem(2 * n + half + 4, 16), w)
-
-    source = (n, lax.div(piece, 2))
+        dy = 2 * core + half
+        dx = lax.rem(z + 10 - dy - lax.div(w, 2), 4)
+        return (4 * lax.rem(y + dy, 4) + lax.rem(x + dx, 4), w)
+
+    source = (n, lax.div(piece_at(x, y), 2))
 
     slab_copy = pltpu.make_async_copy(slab_hbm, slab_ref, local_sem.at[0])
     diag_own = pltpu.make_async_copy(
@@ -166,26 +172,47 @@
         return remote(block, block, rest_send.at[step], rest_recv.at[origin],
                       (w, lax.rem(n + step, 8)))
 
+    line = (y, x)
+
+    def pieces(side, row, first, count):
+        start = 192 * row + 48 * first
+        return (row_b if side else row_a).at[pl.ds(pl.multiple_of(start, 48), 48 * count)]
+
     def part_copy(half, side):
-        p = 2 * n + half
-        p_y, p_x = lax.div(p, 4), lax.rem(p, 4)
-        place = 48 * (4 * p_x + p_y if side else 4 * p_y + p_x)
+        row = lax.rem(target(half)[0], 4) if side else lax.div(target(half)[0], 4)
         return remote(
             col_all.at[pl.ds(pl.multiple_of(192 * n + 96 * half + 48 * side, 48), 48)],
-            (row_b if side else row_a).at[pl.ds(pl.multiple_of(place, 48), 48)],
-            part_send.at[2 * half + side], part_recv.at[side], target(half))
+            pieces(side, row, 0, 1), part_send.at[2 * half + side], part_recv.at[side],
+            target(half))
 
     def one_copy(step, side):
-        buffer, slot = (row_b, slot_b) if side else (row_a, slot_a)
-        block = buffer.at[pl.ds(pl.multiple_of(48 * slot, 48), 48)]
-        return remote(block, block, one_send.at[side, step], one_recv.at[side, step],
-                      along_y(step) if side else along_x(step))
-
-    def two_copy(step, side):
-        buffer, slot = (row_b, piece_x) if side else (row_a, piece_y)
-        block = buffer.at[pl.ds(pl.multiple_of(192 * slot, 192), 192)]
-        return remote(block, block, two_send.at[side, step], two_recv.at[side, step],
-                      along_x(step) if side else along_y(step))
+        return remote(
+            pieces(side, line[side], 0, 1), pieces(side, line[side], 4 - step, 1),
+            one_send.at[side, step], one_recv.at[side, step],
+            along_y(step) if side else along_x(step))
+
+    def across(step, side):
+        return along_x(step) if side else along_y(step)
+
+    def two_copy(step, side, rest):
+        block = pieces(side, line[side], 1, 3) if rest else pieces(side, line[side], 0, 1)
+        return remote(block, block, two_send.at[side, rest, step], two_recv.at[side, rest, step],
+                      across(step, side))
+
+    def relay_copy(side, rest):
+        row = lax.rem(line[side] + 4 - ahead, 4)
+        block = pieces(side, row, 1, 3) if rest else pieces(side, row, 0, 1)
+        return remote(block, block, relay_send.at[side, rest], relay_recv.at[side, rest],
+                      across(ahead, side))
+
+    def wait_two(side, rest, forward):
+        @pl.when(core == (0 if forward else 1))
+        def _():
+            two_copy(1, side, rest).wait_recv()
+
+        @pl.when(core == (1 if forward else 0))
+        def _():
+            two_copy(3, side, rest).wait_recv()
 
     def col_copy(step):
         block = col_all.at[pl.ds(pl.multiple_of(192 * n, 64), 192)]
@@ -219,14 +246,25 @@
         for step in range(1, 8):
             rest_copy(step, n).start()
 
-    for side in range(2):
-        part_copy(0, side).wait_recv()
-    for step in range(1, 4):
-        one_copy(step, 0).start()
-        one_copy(step, 1).start()
-    for step in range(1, 4):
-        col_copy(step).start()
-    twin_copy(0).start()
+    def start_cols():
+        for step in (1, 3, 2):
+            col_copy(step).start()
+        twin_copy(0).start()
+
+    def first_phase():
+        for side in range(2):
+            part_copy(0, side).wait_recv()
+            for step in (1, 3, 2):
+                one_copy(step, side).start()
+            for step in (1, 3):
+                two_copy(step, side, 0).start()
+
+    if COLS_FIRST:
+        start_cols()
+        first_phase()
+    else:
+        first_phase()
+        start_cols()
 
     for origin in range(4):
         @pl.when(n != origin)
@@ -257,9 +295,15 @@
         for side in range(2):
             for step in range(1, 4):
                 one_copy(step, side).wait_recv()
-        for step in range(1, 4):
-            two_copy(step, 0).start()
-            two_copy(step, 1).start()
+            for step in (1, 3):
+                two_copy(step, side, 1).start()
+            wait_two(side, 0, True)
+            relay_copy(side, 0).start()
+
+    def third_phase():
+        for side in range(2):
+            wait_two(side, 1, True)
+            relay_copy(side, 1).start()
 
     def to_twin():
         for step in range(1, 4):
@@ -279,7 +323,7 @@
     below = full_dot(corner, first, LAST)
     beside = full_dot(first, corner, LAST)
     work[128:256, :] = work[128:256, :] - full_dot(below, beside, PLAIN)
-    eliminate(work.at[128:256], inv.at[128:256, 128:256], {TWIN: to_twin})
+    eliminate(work.at[128:256], inv.at[128:256, 128:256], {PHASE_THREE: third_phase, TWIN: to_twin})
     inv[128:256, 0:128] = -full_dot(
         inv[128:256, 128:256], full_dot(below, first, PLAIN), PLAIN)
 
@@ -297,13 +341,17 @@
         col_ref[start : start + 768, 0:256] = high
         col_ref[start : start + 768, 256:512] = low
     for side in range(2):
-        for step in range(1, 4):
-            two_copy(step, side).wait_recv()
+        wait_two(side, 0, False)
+        wait_two(side, 1, False)
+        relay_copy(side, 0).wait_recv()
+        relay_copy(side, 1).wait_recv()
         high, low = solve((row_b if side else row_a)[...])
         for slot in range(16):
-            place = 96 * (4 * (slot % 4) + slot // 4) + 48 if side else 96 * slot
-            row_ref[place : place + 48, 0:256] = high[48 * slot : 48 * slot + 48]
-            row_ref[place : place + 48, 256:512] = low[48 * slot : 48 * slot + 48]
+            row, other = slot // 4, lax.rem(line[1 - side] + slot % 4, 4)
+            place = 96 * (piece_at(row, other) if side else piece_at(other, row)) + 48 * side
+            place = pl.ds(pl.multiple_of(place, 48), 48)
+            row_ref[place, 0:256] = high[48 * slot : 48 * slot + 48]
+            row_ref[place, 256:512] = low[48 * slot : 48 * slot + 48]
 
     @pl.when(n < 4)
     def _():
@@ -322,10 +370,14 @@
             for side in range(2):
                 part_copy(half, side).wait_send()
 
+    for side in range(2):
+        for step in range(1, 4):
+            one_copy(step, side).wait_send()
+        for rest in range(2):
+            two_copy(1, side, rest).wait_send()
+            two_copy(3, side, rest).wait_send()
+            relay_copy(side, rest).wait_send()
     for step in range(1, 4):
-        for side in range(2):
-            one_copy(step, side).wait_send()
-            two_copy(step, side).wait_send()
         col_copy(step).wait_send()
     for step in range(4):
         twin_copy(step).wait_send()
@@ -353,7 +405,7 @@
             pltpu.VMEM((256, 256), jnp.float32),
             sems((3,)), sems((8,)), sems((8,)), sems((8,)), sems((8,)), sems((4,)), sems((4,)),
             sems((4,)), sems((4,)), sems((4,)), sems((2,)), sems((2, 4)), sems((2, 4)),
-            sems((2, 4)), sems((2, 4)),
+            sems((2, 2, 4)), sems((2, 2, 4)), sems((2, 2)), sems((2, 2)),
         ],
         compiler_params=pltpu.CompilerParams(
             collective_id=0, has_side_effects=True, vmem_limit_bytes=28 << 20),

time: 41 us -> 37.5 us (0.915)
  Pallas kernels: 40.9 us -> 37.4 us
    pallas_call x1, Pallas kernels: 35.2 us -> 31.8 us  [gather_and_solve(): pl.pallas_call(gather_kernel, out_shape=(out, out, jax.ShapeDtypeStruct(s...]
where the time goes in v3:
time: 37.5 us; the launch traced here: 37.4 us
  Pallas kernels  37.4 us (100%)
    pallas_call x1, Pallas kernels, gather_and_solve(): pl.pallas_call(gather_kernel, out_shape=(out, out, jax.ShapeDtypeStruct(s...  31.8 us
    pallas_call x1, Pallas kernels, update(): pl.pallas_call(update_kernel, out_shape=jax.ShapeDtypeStruct(slab.shape,...  5.62 us

profile of v3, /device:TPU:1, one launch (start us, length us, event | category | flops | bytes accessed | tf_op | source)
XLA Modules:
  0.0 37.4 jit_solution(8618325643422615019)
XLA Ops:
  0.0 31.8 %gather_and_solve.1 = (bf16[1536,512]{1,0:T(8,128)(2,1)S(1)}, bf16[1536,512]{1,0:T(8,128)(2,1)S(1)}, f32[1536,1536]{1,0:T(8,128)S(1)}) custom-call(f32[32,256]{1,0:T(8,128)} %diag_hbm.1, f32[192,256]{1,0:T(8,128)} %panel_hbm.1, f32[1536,1536]{1,0:T(8,128)} %slab_hbm.1), custom_call_target="tpu_custom_call" | custom-call | tf_op jit(solution)/shard_map/gather_and_solve/pallas_call | solution.py:393
  31.8 5.6 %update.1 = f32[1536,1536]{1,0:T(8,128)} custom-call(bf16[1536,512]{1,0:T(8,128)(2,1)S(1)} %get-tuple-element.8.row_ref, bf16[1536,512]{1,0:T(8,128)(2,1)S(1)} %get-tuple-element.9.col_ref, f32[1536,1536]{1,0:T(8,128)S(1)} %get-tuple-element.10.slab_ref), custom_call_target="tpu_custom_call" | custom-call | tf_op jit(solution)/shard_map/update/pallas_call | solution.py:441

commit v4 on v3

--- a/solution.py
+++ b/solution.py
@@ -9,7 +9,7 @@
 
 unit_gamma = 65538.0 * 2.0 ** (-24) / (1.0 - 65538.0 * 2.0 ** (-24))
 MESH = pl.DeviceIdType.MESH
-PHASE_TWO, PHASE_THREE, TWIN, COLS_FIRST = 6, 4, 8, False
+PHASE_TWO, TWIN = 8, 10
 LAST = (((1,), (1,)), ((), ()))
 PLAIN = (((1,), (0,)), ((), ()))
 
@@ -138,6 +138,89 @@
         signal(target(1))
 
     slab_copy.start()
+    @pl.when(w < 8)
+    def _():
+        pl.semaphore_wait(barrier, 16)
+
+    @pl.when(w >= 8)
+    def _():
+        pl.semaphore_wait(barrier, 14)
+
+    def remote(src, dst, send, recv, device):
+        return pltpu.make_async_remote_copy(
+            src, dst, send, recv, device_id=device, device_id_type=MESH)
+
+    def corner_copy(step, origin):
+        block = diag_all.at[pl.ds(pl.multiple_of(32 * origin, 32), 32), 0:128]
+        return remote(block, block, diag_send.at[step], diag_recv.at[origin],
+                      (w, lax.rem(n + step, 8)))
+
+    def trace_copy(step, origin):
+        return remote(traces.at[origin], traces.at[origin], diag_send.at[step],
+                      diag_recv.at[origin], (w, lax.rem(n + step, 8)))
+
+    def rest_copy(step, origin):
+        block = diag_all.at[pl.ds(pl.multiple_of(32 * origin, 32), 32)]
+        return remote(block, block, rest_send.at[step], rest_recv.at[origin],
+                      (w, lax.rem(n + step, 8)))
+
+    line = (y, x)
+
+    def pieces(side, row, first, count):
+        start = 192 * row + 48 * first
+        return (row_b if side else row_a).at[pl.ds(pl.multiple_of(start, 48), 48 * count)]
+
+    def part_copy(half, side):
+        row = lax.rem(target(half)[0], 4) if side else lax.div(target(half)[0], 4)
+        return remote(
+            col_all.at[pl.ds(pl.multiple_of(192 * n + 96 * half + 48 * side, 48), 48)],
+            pieces(side, row, 0, 1), part_send.at[2 * half + side], part_recv.at[side],
+            target(half))
+
+    def one_copy(step, side):
+        return remote(
+            pieces(side, line[side], 0, 1), pieces(side, line[side], 4 - step, 1),
+            one_send.at[side, step], one_recv.at[side, step],
+            along_y(step) if side else along_x(step))
+
+    def across(step, side):
+        return along_x(step) if side else along_y(step)
+
+    def two_copy(step, side, rest):
+        block = pieces(side, line[side], 1, 3) if rest else pieces(side, line[side], 0, 1)
+        return remote(block, block, two_send.at[side, rest, step], two_recv.at[side, rest, step],
+                      across(step, side))
+
+    def relay_copy(side):
+        block = pieces(side, lax.rem(line[side] + 4 - ahead, 4), 0, 1)
+        return remote(block, block, relay_send.at[side], relay_recv.at[side], across(ahead, side))
+
+    def wait_two(side, forward):
+        @pl.when(core == (0 if forward else 1))
+        def _():
+            two_copy(1, side, 0).wait_recv()
+
+        @pl.when(core == (1 if forward else 0))
+        def _():
+            two_copy(3, side, 0).wait_recv()
+
+    def col_copy(step):
+        block = col_all.at[pl.ds(pl.multiple_of(192 * n, 64), 192)]
+        return remote(block, block, col_send.at[step], col_recv.at[step], along_z(step))
+
+    def twin_copy(step):
+        origin = 2 * lax.rem(z + 4 - step, 4) + core
+        block = col_all.at[pl.ds(pl.multiple_of(192 * origin, 64), 192)]
+        return remote(block, block, twin_send.at[step], twin_recv.at[step], twin)
+
+    panel_own.wait()
+
+    @pl.when(w < 8)
+    def _():
+        for half in range(2):
+            for side in range(2):
+                part_copy(half, side).start()
+
     diag_own.wait()
     row_id = lax.broadcasted_iota(jnp.int32, (32, 256), 0)
     col_id = lax.broadcasted_iota(jnp.int32, (32, 256), 1)
@@ -146,83 +229,6 @@
     own = own[:, 0:128] + own[:, 128:256]
     traces[n] = jnp.sum(own, axis=0, keepdims=True)
 
-    @pl.when(w < 8)
-    def _():
-        pl.semaphore_wait(barrier, 16)
-
-    @pl.when(w >= 8)
-    def _():
-        pl.semaphore_wait(barrier, 14)
-
-    def remote(src, dst, send, recv, device):
-        return pltpu.make_async_remote_copy(
-            src, dst, send, recv, device_id=device, device_id_type=MESH)
-
-    def corner_copy(step, origin):
-        block = diag_all.at[pl.ds(pl.multiple_of(32 * origin, 32), 32), 0:128]
-        return remote(block, block, diag_send.at[step], diag_recv.at[origin],
-                      (w, lax.rem(n + step, 8)))
-
-    def trace_copy(step, origin):
-        return remote(traces.at[origin], traces.at[origin], diag_send.at[step],
-                      diag_recv.at[origin], (w, lax.rem(n + step, 8)))
-
-    def rest_copy(step, origin):
-        block = diag_all.at[pl.ds(pl.multiple_of(32 * origin, 32), 32)]
-        return remote(block, block, rest_send.at[step], rest_recv.at[origin],
-                      (w, lax.rem(n + step, 8)))
-
-    line = (y, x)
-
-    def pieces(side, row, first, count):
-        start = 192 * row + 48 * first
-        return (row_b if side else row_a).at[pl.ds(pl.multiple_of(start, 48), 48 * count)]
-
-    def part_copy(half, side):
-        row = lax.rem(target(half)[0], 4) if side else lax.div(target(half)[0], 4)
-        return remote(
-            col_all.at[pl.ds(pl.multiple_of(192 * n + 96 * half + 48 * side, 48), 48)],
-            pieces(side, row, 0, 1), part_send.at[2 * half + side], part_recv.at[side],
-            target(half))
-
-    def one_copy(step, side):
-        return remote(
-            pieces(side, line[side], 0, 1), pieces(side, line[side], 4 - step, 1),
-            one_send.at[side, step], one_recv.at[side, step],
-            along_y(step) if side else along_x(step))
-
-    def across(step, side):
-        return along_x(step) if side else along_y(step)
-
-    def two_copy(step, side, rest):
-        block = pieces(side, line[side], 1, 3) if rest else pieces(side, line[side], 0, 1)
-        return remote(block, block, two_send.at[side, rest, step], two_recv.at[side, rest, step],
-                      across(step, side))
-
-    def relay_copy(side, rest):
-        row = lax.rem(line[side] + 4 - ahead, 4)
-        block = pieces(side, row, 1, 3) if rest else pieces(side, row, 0, 1)
-        return remote(block, block, relay_send.at[side, rest], relay_recv.at[side, rest],
-                      across(ahead, side))
-
-    def wait_two(side, rest, forward):
-        @pl.when(core == (0 if forward else 1))
-        def _():
-            two_copy(1, side, rest).wait_recv()
-
-        @pl.when(core == (1 if forward else 0))
-        def _():
-            two_copy(3, side, rest).wait_recv()
-
-    def col_copy(step):
-        block = col_all.at[pl.ds(pl.multiple_of(192 * n, 64), 192)]
-        return remote(block, block, col_send.at[step], col_recv.at[step], along_z(step))
-
-    def twin_copy(step):
-        origin = 2 * lax.rem(z + 4 - step, 4) + core
-        block = col_all.at[pl.ds(pl.multiple_of(192 * origin, 64), 192)]
-        return remote(block, block, twin_send.at[step], twin_recv.at[step], twin)
-
     @pl.when(n < 4)
     def _():
         for step in range(1, 8):
@@ -232,14 +238,6 @@
     def _():
         for step in range(1, 8):
             trace_copy(step, n).start()
-
-    panel_own.wait()
-
-    @pl.when(w < 8)
-    def _():
-        for half in range(2):
-            for side in range(2):
-                part_copy(half, side).start()
 
     @pl.when(n >= 4)
     def _():
@@ -259,12 +257,8 @@
             for step in (1, 3):
                 two_copy(step, side, 0).start()
 
-    if COLS_FIRST:
-        start_cols()
-        first_phase()
-    else:
-        first_phase()
-        start_cols()
+    start_cols()
+    first_phase()
 
     for origin in range(4):
         @pl.when(n != origin)
@@ -295,15 +289,11 @@
         for side in range(2):
             for step in range(1, 4):
                 one_copy(step, side).wait_recv()
-            for step in (1, 3):
+            for step in (1, 3, 2):
                 two_copy(step, side, 1).start()
-            wait_two(side, 0, True)
-            relay_copy(side, 0).start()
-
-    def third_phase():
         for side in range(2):
-            wait_two(side, 1, True)
-            relay_copy(side, 1).start()
+            wait_two(side, True)
+            relay_copy(side).start()
 
     def to_twin():
         for step in range(1, 4):
@@ -323,7 +313,7 @@
     below = full_dot(corner, first, LAST)
     beside = full_dot(first, corner, LAST)
     work[128:256, :] = work[128:256, :] - full_dot(below, beside, PLAIN)
-    eliminate(work.at[128:256], inv.at[128:256, 128:256], {PHASE_THREE: third_phase, TWIN: to_twin})
+    eliminate(work.at[128:256], inv.at[128:256, 128:256], {TWIN: to_twin})
     inv[128:256, 0:128] = -full_dot(
         inv[128:256, 128:256], full_dot(below, first, PLAIN), PLAIN)
 
@@ -341,10 +331,10 @@
         col_ref[start : start + 768, 0:256] = high
         col_ref[start : start + 768, 256:512] = low
     for side in range(2):
-        wait_two(side, 0, False)
-        wait_two(side, 1, False)
-        relay_copy(side, 0).wait_recv()
-        relay_copy(side, 1).wait_recv()
+        wait_two(side, False)
+        relay_copy(side).wait_recv()
+        for step in range(1, 4):
+            two_copy(step, side, 1).wait_recv()
         high, low = solve((row_b if side else row_a)[...])
         for slot in range(16):
             row, other = slot // 4, lax.rem(line[1 - side] + slot % 4, 4)
@@ -373,10 +363,10 @@
     for side in range(2):
         for step in range(1, 4):
             one_copy(step, side).wait_send()
-        for rest in range(2):
-            two_copy(1, side, rest).wait_send()
-            two_copy(3, side, rest).wait_send()
-            relay_copy(side, rest).wait_send()
+            two_copy(step, side, 1).wait_send()
+        two_copy(1, side, 0).wait_send()
+        two_copy(3, side, 0).wait_send()
+        relay_copy(side).wait_send()
     for step in range(1, 4):
         col_copy(step).wait_send()
     for step in range(4):
@@ -405,7 +395,7 @@
             pltpu.VMEM((256, 256), jnp.float32),
             sems((3,)), sems((8,)), sems((8,)), sems((8,)), sems((8,)), sems((4,)), sems((4,)),
             sems((4,)), sems((4,)), sems((4,)), sems((2,)), sems((2, 4)), sems((2, 4)),
-            sems((2, 2, 4)), sems((2, 2, 4)), sems((2, 2)), sems((2, 2)),
+            sems((2, 2, 4)), sems((2, 2, 4)), sems((2,)), sems((2,)),
         ],
         compiler_params=pltpu.CompilerParams(
             collective_id=0, has_side_effects=True, vmem_limit_bytes=28 << 20),

time: 37.5 us -> 35 us (0.933)
  Pallas kernels: 37.4 us -> 34.6 us
    pallas_call x1, Pallas kernels: 31.8 us -> 29 us  [gather_and_solve(): pl.pallas_call(gather_kernel, out_shape=(out, out, jax.ShapeDtypeStruct(s...]
where the time goes in v4:
time: 35 us; the launch traced here: 34.6 us
  Pallas kernels  34.6 us (99%)
    pallas_call x1, Pallas kernels, gather_and_solve(): pl.pallas_call(gather_kernel, out_shape=(out, out, jax.ShapeDtypeStruct(s...  29 us
    pallas_call x1, Pallas kernels, update(): pl.pallas_call(update_kernel, out_shape=jax.ShapeDtypeStruct(slab.shape,...  5.62 us

profile of v4, /device:TPU:1, one launch (start us, length us, event | category | flops | bytes accessed | tf_op | source)
XLA Modules:
  0.0 34.6 jit_solution(2951087784330724575)
XLA Ops:
  0.0 29.0 %gather_and_solve.1 = (bf16[1536,512]{1,0:T(8,128)(2,1)S(1)}, bf16[1536,512]{1,0:T(8,128)(2,1)S(1)}, f32[1536,1536]{1,0:T(8,128)S(1)}) custom-call(f32[32,256]{1,0:T(8,128)} %diag_hbm.1, f32[192,256]{1,0:T(8,128)} %panel_hbm.1, f32[1536,1536]{1,0:T(8,128)} %slab_hbm.1), custom_call_target="tpu_custom_call" | custom-call | tf_op jit(solution)/shard_map/gather_and_solve/pallas_call | solution.py:383
  29.0 5.6 %update.1 = f32[1536,1536]{1,0:T(8,128)} custom-call(bf16[1536,512]{1,0:T(8,128)(2,1)S(1)} %get-tuple-element.8.row_ref, bf16[1536,512]{1,0:T(8,128)(2,1)S(1)} %get-tuple-element.9.col_ref, f32[1536,1536]{1,0:T(8,128)S(1)} %get-tuple-element.10.slab_ref), custom_call_target="tpu_custom_call" | custom-call | tf_op jit(solution)/shard_map/update/pallas_call | solution.py:431

commit v5 on v4

--- a/solution.py
+++ b/solution.py
@@ -405,25 +405,22 @@
 
 def update_kernel(row_ref, col_ref, slab_ref, out_hbm, buffer, sem):
     rows, cols = slab_ref.shape
-    tall, broad, depth = 768, 512, 3
-    tiles = [(i, j) for i in range(0, rows, tall) for j in range(0, cols, broad)]
-
-    def out_copy(t):
-        i, j = tiles[t]
-        return pltpu.make_async_copy(
-            buffer.at[t % depth], out_hbm.at[pl.ds(i, tall), pl.ds(j, broad)], sem.at[t % depth])
-
-    for t, (i, j) in enumerate(tiles):
-        if t >= depth:
-            out_copy(t - depth).wait()
-        high, low = row_ref[i : i + tall, 0:256], row_ref[i : i + tall, 256:512]
-        col_high, col_low = col_ref[j : j + broad, 0:256], col_ref[j : j + broad, 256:512]
-        product = (half_dot(high, col_high, LAST) + half_dot(high, col_low, LAST)
-                   + half_dot(low, col_high, LAST))
-        buffer[t % depth] = slab_ref[i : i + tall, j : j + broad] - product
-        out_copy(t).start()
-    for t in range(len(tiles) - depth, len(tiles)):
-        out_copy(t).wait()
+    tall, broad = 384, 512
+    copies = []
+    for i in range(0, rows, tall):
+        for j in range(0, cols, broad):
+            t = len(copies)
+            high, low = row_ref[i : i + tall, 0:256], row_ref[i : i + tall, 256:512]
+            col_high, col_low = col_ref[j : j + broad, 0:256], col_ref[j : j + broad, 256:512]
+            product = (half_dot(high, col_high, LAST) + half_dot(high, col_low, LAST)
+                       + half_dot(low, col_high, LAST))
+            buffer[i : i + tall, j : j + broad] = slab_ref[i : i + tall, j : j + broad] - product
+            copies.append(pltpu.make_async_copy(
+                buffer.at[pl.ds(i, tall), pl.ds(j, broad)],
+                out_hbm.at[pl.ds(i, tall), pl.ds(j, broad)], sem.at[t]))
+            copies[-1].start()
+    for copy in copies:
+        copy.wait()
 
 
 def update(row_panel, col_panel, slab):
@@ -433,7 +430,7 @@
         out_shape=jax.ShapeDtypeStruct(slab.shape, jnp.float32),
         in_specs=[vmem, vmem, vmem],
         out_specs=pl.BlockSpec(memory_space=pltpu.HBM),
-        scratch_shapes=[pltpu.VMEM((3, 768, 512), jnp.float32), pltpu.SemaphoreType.DMA((3,))],
+        scratch_shapes=[pltpu.VMEM(slab.shape, jnp.float32), pltpu.SemaphoreType.DMA((12,))],
         compiler_params=pltpu.CompilerParams(vmem_limit_bytes=24 << 20),
         name="update",
     )(row_panel, col_panel, slab)

time: 35 us -> 34.2 us (0.977)
  Pallas kernels: 34.6 us -> 33.8 us
    pallas_call x1, Pallas kernels: 5.62 us -> 4.84 us  [update(): pl.pallas_call(update_kernel, out_shape=jax.ShapeDtypeStruct(slab.shape,...]
where the time goes in v5:
time: 34.2 us; the launch traced here: 33.8 us
  Pallas kernels  33.8 us (99%)
    pallas_call x1, Pallas kernels, gather_and_solve(): pl.pallas_call(gather_kernel, out_shape=(out, out, jax.ShapeDtypeStruct(s...  29 us
    pallas_call x1, Pallas kernels, update(): pl.pallas_call(update_kernel, out_shape=jax.ShapeDtypeStruct(slab.shape,...  4.84 us

profile of v5, /device:TPU:1, one launch (start us, length us, event | category | flops | bytes accessed | tf_op | source)
XLA Modules:
  0.0 33.8 jit_solution(201711103177908608)
XLA Ops:
  0.0 29.0 %gather_and_solve.1 = (bf16[1536,512]{1,0:T(8,128)(2,1)S(1)}, bf16[1536,512]{1,0:T(8,128)(2,1)S(1)}, f32[1536,1536]{1,0:T(8,128)S(1)}) custom-call(f32[32,256]{1,0:T(8,128)} %diag_hbm.1, f32[192,256]{1,0:T(8,128)} %panel_hbm.1, f32[1536,1536]{1,0:T(8,128)} %slab_hbm.1), custom_call_target="tpu_custom_call" | custom-call | tf_op jit(solution)/shard_map/gather_and_solve/pallas_call | solution.py:383
  29.0 4.8 %update.1 = f32[1536,1536]{1,0:T(8,128)} custom-call(bf16[1536,512]{1,0:T(8,128)(2,1)S(1)} %get-tuple-element.8.row_ref, bf16[1536,512]{1,0:T(8,128)(2,1)S(1)} %get-tuple-element.9.col_ref, f32[1536,1536]{1,0:T(8,128)S(1)} %get-tuple-element.10.slab_ref), custom_call_target="tpu_custom_call" | custom-call | tf_op jit(solution)/shard_map/update/pallas_call | solution.py:428

commit v6 on v5

--- a/solution.py
+++ b/solution.py
@@ -9,7 +9,7 @@
 
 unit_gamma = 65538.0 * 2.0 ** (-24) / (1.0 - 65538.0 * 2.0 ** (-24))
 MESH = pl.DeviceIdType.MESH
-PHASE_TWO, TWIN = 8, 10
+PHASE_TWO, TWIN = 10, 10
 LAST = (((1,), (1,)), ((), ()))
 PLAIN = (((1,), (0,)), ((), ()))
 
@@ -330,18 +330,27 @@
         high, low = solve(col_all[start : start + 768, :])
         col_ref[start : start + 768, 0:256] = high
         col_ref[start : start + 768, 256:512] = low
+    def place_rows(side, slots, halved):
+        for k, (row, step) in enumerate(slots):
+            row, other = lax.rem(line[side] + row, 4), lax.rem(line[1 - side] + step, 4)
+            place = 96 * (piece_at(row, other) if side else piece_at(other, row)) + 48 * side
+            place = pl.ds(pl.multiple_of(place, 48), 48)
+            row_ref[place, 0:256] = halved[0][48 * k : 48 * k + 48]
+            row_ref[place, 256:512] = halved[1][48 * k : 48 * k + 48]
+
+    early = solve(jnp.concatenate([pieces(side, line[side], 0, 4)[...] for side in range(2)], axis=0))
+    for side in range(2):
+        rows = slice(192 * side, 192 * side + 192)
+        place_rows(side, [(0, j) for j in range(4)], (early[0][rows], early[1][rows]))
+
     for side in range(2):
         wait_two(side, False)
         relay_copy(side).wait_recv()
         for step in range(1, 4):
             two_copy(step, side, 1).wait_recv()
-        high, low = solve((row_b if side else row_a)[...])
-        for slot in range(16):
-            row, other = slot // 4, lax.rem(line[1 - side] + slot % 4, 4)
-            place = 96 * (piece_at(row, other) if side else piece_at(other, row)) + 48 * side
-            place = pl.ds(pl.multiple_of(place, 48), 48)
-            row_ref[place, 0:256] = high[48 * slot : 48 * slot + 48]
-            row_ref[place, 256:512] = low[48 * slot : 48 * slot + 48]
+        late = [pieces(side, lax.rem(line[side] + i, 4), 0, 4)[...] for i in range(1, 4)]
+        place_rows(side, [(i, j) for i in range(1, 4) for j in range(4)],
+                   solve(jnp.concatenate(late, axis=0)))
 
     @pl.when(n < 4)
     def _():

time: 34.2 us -> 33.8 us (0.988)
  no operation moved by 1% of the time
where the time goes in v6:
time: 33.8 us; the launch traced here: 33.7 us
  Pallas kernels  33.7 us (100%)
    pallas_call x1, Pallas kernels, gather_and_solve(): pl.pallas_call(gather_kernel, out_shape=(out, out, jax.ShapeDtypeStruct(s...  28.9 us
    pallas_call x1, Pallas kernels, update(): pl.pallas_call(update_kernel, out_shape=jax.ShapeDtypeStruct(slab.shape,...  4.84 us

profile of v6, /device:TPU:1, one launch (start us, length us, event | category | flops | bytes accessed | tf_op | source)
XLA Modules:
  0.0 33.7 jit_solution(4927714880218385628)
XLA Ops:
  0.0 28.9 %gather_and_solve.1 = (bf16[1536,512]{1,0:T(8,128)(2,1)S(1)}, bf16[1536,512]{1,0:T(8,128)(2,1)S(1)}, f32[1536,1536]{1,0:T(8,128)S(1)}) custom-call(f32[32,256]{1,0:T(8,128)} %diag_hbm.1, f32[192,256]{1,0:T(8,128)} %panel_hbm.1, f32[1536,1536]{1,0:T(8,128)} %slab_hbm.1), custom_call_target="tpu_custom_call" | custom-call | tf_op jit(solution)/shard_map/gather_and_solve/pallas_call | solution.py:392
  28.9 4.8 %update.1 = f32[1536,1536]{1,0:T(8,128)} custom-call(bf16[1536,512]{1,0:T(8,128)(2,1)S(1)} %get-tuple-element.8.row_ref, bf16[1536,512]{1,0:T(8,128)(2,1)S(1)} %get-tuple-element.9.col_ref, f32[1536,1536]{1,0:T(8,128)S(1)} %get-tuple-element.10.slab_ref), custom_call_target="tpu_custom_call" | custom-call | tf_op jit(solution)/shard_map/update/pallas_call | solution.py:437

commit v7 on v6

--- a/solution.py
+++ b/solution.py
@@ -222,13 +222,6 @@
                 part_copy(half, side).start()
 
     diag_own.wait()
-    row_id = lax.broadcasted_iota(jnp.int32, (32, 256), 0)
-    col_id = lax.broadcasted_iota(jnp.int32, (32, 256), 1)
-    own = diag_all[pl.ds(pl.multiple_of(32 * n, 32), 32), :]
-    own = jnp.where(col_id == row_id + 32 * n, own, 0.0)
-    own = own[:, 0:128] + own[:, 128:256]
-    traces[n] = jnp.sum(own, axis=0, keepdims=True)
-
     @pl.when(n < 4)
     def _():
         for step in range(1, 8):
@@ -236,6 +229,12 @@
 
     @pl.when(n >= 4)
     def _():
+        row_id = lax.broadcasted_iota(jnp.int32, (32, 256), 0)
+        col_id = lax.broadcasted_iota(jnp.int32, (32, 256), 1)
+        own = diag_all[pl.ds(pl.multiple_of(32 * n, 32), 32), :]
+        own = jnp.where(col_id == row_id + 32 * n, own, 0.0)
+        own = own[:, 0:128] + own[:, 128:256]
+        traces[n] = jnp.sum(own, axis=0, keepdims=True)
         for step in range(1, 8):
             trace_copy(step, n).start()
 

time: 33.8 us -> 33.8 us (level)
  no operation moved by 1% of the time
where the time goes in v7:
time: 33.8 us; the launch traced here: 33.7 us
  Pallas kernels  33.7 us (100%)
    pallas_call x1, Pallas kernels, gather_and_solve(): pl.pallas_call(gather_kernel, out_shape=(out, out, jax.ShapeDtypeStruct(s...  28.9 us
    pallas_call x1, Pallas kernels, update(): pl.pallas_call(update_kernel, out_shape=jax.ShapeDtypeStruct(slab.shape,...  4.84 us

profile of v7, /device:TPU:1, one launch (start us, length us, event | category | flops | bytes accessed | tf_op | source)
XLA Modules:
  0.0 33.7 jit_solution(3361331343680164661)
XLA Ops:
  0.0 28.9 %gather_and_solve.1 = (bf16[1536,512]{1,0:T(8,128)(2,1)S(1)}, bf16[1536,512]{1,0:T(8,128)(2,1)S(1)}, f32[1536,1536]{1,0:T(8,128)S(1)}) custom-call(f32[32,256]{1,0:T(8,128)} %diag_hbm.1, f32[192,256]{1,0:T(8,128)} %panel_hbm.1, f32[1536,1536]{1,0:T(8,128)} %slab_hbm.1), custom_call_target="tpu_custom_call" | custom-call | tf_op jit(solution)/shard_map/gather_and_solve/pallas_call | solution.py:391
  28.9 4.8 %update.1 = f32[1536,1536]{1,0:T(8,128)} custom-call(bf16[1536,512]{1,0:T(8,128)(2,1)S(1)} %get-tuple-element.8.row_ref, bf16[1536,512]{1,0:T(8,128)(2,1)S(1)} %get-tuple-element.9.col_ref, f32[1536,1536]{1,0:T(8,128)S(1)} %get-tuple-element.10.slab_ref), custom_call_target="tpu_custom_call" | custom-call | tf_op jit(solution)/shard_map/update/pallas_call | solution.py:436
